TPU v7x, 256 devices: a whole 4x4x8 slice. The times are simulated.
256 devices in a mesh: gx: 16 (over x, z_hi), gy: 8 (over y, core), ga: 2 (over z_lo).
Axes of the slice: x: 4, y: 4, z: 8 (z_hi: 4, z_lo: 2; z = z_hi * 2 + z_lo), core: 2. Of those that a mesh axis runs over, the one named last changes fastest.
Arguments:
- head: float32 [16, 256, 8192], P(None, 'gx', ('gy', 'ga')), may hold values from -6 to 6
- conductivity: float32 [16, 256, 8192], P(None, 'gx', ('gy', 'ga')), may hold values from 0.1 to 10
- root_layer: int32 [256, 8192], P('gx', ('gy', 'ga')), may hold values from 0 to 15
- veg_type: int32 [256, 8192], P('gx', ('gy', 'ga')), may hold values from 0 to 16
- uptake_rate: float32 [17], replicated, may hold values from 0.2 to 2
- depth: float32 [256, 8192], P('gx'), may hold values from 0.05 to 2
- conveyance: float32 [256, 8192], P('gx'), may hold values from 0.2 to 5
- elevation: float32 [256, 8192], P('gx'), may hold values from -3 to 3
- land_mask: int32 [256, 8192], P('gx'), may hold values 0 or 1
Outputs:
- new_head: float32 [16, 256, 8192], P(None, 'gx', ('gy', 'ga'))
- new_depth: float32 [256, 8192], P('gx')
All inputs are finite; a program needn't handle non-finite values. No bound on the sum of `land_mask` on one device may be relied on, other than what follows from the above.
Results may differ from a plain program's by a relative error of at most 0.0003.
Values sent between devices are 32-bit elements; how exact they have to be, the bound alone decides.
A program may use at most 64 MiB of HBM per device.

v0:
```python
import jax
import jax.numpy as jnp
from jax import lax
from jax.sharding import PartitionSpec as P

NVEG = 17
SSW = 4
exchange_coef = 0.5
storage_coef = 0.5


def with_halo(cells, sides, width):
    for axis, dim in sides:
        count = lax.axis_size(axis)
        ends = count - 1
        head = lax.slice_in_dim(cells, 0, width, axis=dim)
        tail = lax.slice_in_dim(cells, cells.shape[dim] - width, cells.shape[dim], axis=dim)
        cells = jnp.concatenate(
            [
                lax.ppermute(tail, axis, [(i, (i + 1) % count) for i in range(ends)]),
                cells,
                lax.ppermute(head, axis, [((i + 1) % count, i) for i in range(ends)]),
            ],
            axis=dim,
        )
    return cells


def harmonic(first, second):
    total = first + second
    return 2.0 * first * second / jnp.where(total > 0, total, 1.0)


def lateral(field_ext, coef_ext):
    center = coef_ext[..., 1:-1, 1:-1]
    wsum = jnp.zeros_like(center)
    nsum = jnp.zeros_like(center)
    for rows, cols in (
        (slice(2, None), slice(1, -1)),
        (slice(None, -2), slice(1, -1)),
        (slice(1, -1), slice(2, None)),
        (slice(1, -1), slice(None, -2)),
    ):
        weight = harmonic(center, coef_ext[..., rows, cols])
        wsum = wsum + weight
        nsum = nsum + weight * field_ext[..., rows, cols]
    return (wsum, nsum)


def guarded(numer, denom):
    return jnp.where(denom > 0, numer / jnp.where(denom > 0, denom, 1.0), 0.0)


def surface_sweep(depth_ext, drag_ext, bed_ext, base, diag):
    wsum, nsum = lateral(depth_ext + bed_ext, drag_ext)
    bed = bed_ext[1:-1, 1:-1]
    return guarded(base + nsum - wsum * bed, diag + wsum)


def soil_sweep(head_ext, cond_ext, base, diag):
    cond = cond_ext[:, 1:-1, 1:-1]
    inner = head_ext[:, 1:-1, 1:-1]
    wsum, nsum = lateral(head_ext, cond_ext)
    vertical = harmonic(cond[:-1], cond[1:])
    blank = jnp.zeros_like(cond[:1])
    down = jnp.concatenate([vertical, blank], axis=0)
    upward = jnp.concatenate([blank, vertical], axis=0)
    below = jnp.concatenate([inner[1:], blank], axis=0)
    above = jnp.concatenate([blank, inner[:-1]], axis=0)
    numer = base + nsum + down * (below - 1.0) + upward * (above + 1.0)
    return guarded(numer, diag + wsum + down + upward)


def widen_cols(stacked, width):
    pads = [(0, 0)] * (stacked.ndim - 1) + [(width, width)]
    return jnp.pad(stacked, pads)


def body(
    head, conductivity, root_layer, veg_type, uptake_rate, depth, conveyance, elevation, land_mask
):
    layers_here, rows_here, cols_here = head.shape
    offset = lax.axis_index(("gy", "ga")) * cols_here
    coupling_rows = exchange_coef * land_mask.astype(jnp.float32)
    coupling = lax.dynamic_slice_in_dim(coupling_rows, offset, cols_here, 1)
    top = head[0]
    top_rows = lax.all_gather(top, ("gy", "ga"), axis=1, tiled=True)
    drag = conveyance * jnp.power(depth, 5.0 / 3.0)
    sbase = depth + coupling_rows * top_rows
    sdiag = 1.0 + coupling_rows
    opened = with_halo(jnp.stack([depth, drag, elevation]), (("gx", 1),), 1)
    opened = widen_cols(opened, 1)
    drag_ext = opened[1]
    bed_ext = opened[2]
    level = surface_sweep(opened[0], drag_ext, bed_ext, sbase, sdiag)
    for sweep in range(SSW - 1):
        level_ext = widen_cols(with_halo(level, (("gx", 0),), 1), 1)
        level = surface_sweep(level_ext, drag_ext, bed_ext, sbase, sdiag)
    level_here = lax.dynamic_slice_in_dim(level, offset, cols_here, 1)
    kinds = jnp.arange(NVEG, dtype=jnp.int32)[:, None, None]
    rate = jnp.sum(jnp.where(veg_type[None] == kinds, uptake_rate[:, None, None], 0.0), axis=0)
    layers = jnp.arange(layers_here, dtype=jnp.int32)[:, None, None]
    inside = (layers <= root_layer[None]).astype(jnp.float32)
    sink = rate[None] * inside / (root_layer[None].astype(jnp.float32) + 1.0)
    base = storage_coef * head - sink
    base = base.at[0].add(coupling * level_here)
    diag = jnp.full(head.shape, storage_coef, jnp.float32)
    diag = diag.at[0].add(coupling)
    opened = with_halo(jnp.stack([head, conductivity]), (("gx", 2), (("gy", "ga"), 3)), 1)
    cond_ext = opened[1]
    current = soil_sweep(opened[0], cond_ext, base, diag)
    head_ext = with_halo(current, (("gx", 1), (("gy", "ga"), 2)), 1)
    current = soil_sweep(head_ext, cond_ext, base, diag)
    return (current, level)


def solution(mesh):
    return jax.shard_map(
        body,
        mesh=mesh,
        in_specs=(
            P(None, "gx", ("gy", "ga")),
            P(None, "gx", ("gy", "ga")),
            P("gx", ("gy", "ga")),
            P("gx", ("gy", "ga")),
            P(),
            P("gx", None),
            P("gx", None),
            P("gx", None),
            P("gx", None),
        ),
        out_specs=(P(None, "gx", ("gy", "ga")), P("gx", None)),
        check_vma=False,
    )
```

profile of v0, /device:TPU:34, one launch (start us, length us, event | category | flops | bytes accessed | tf_op | source)
XLA Modules:
  0.0 151.8 jit_solution(12704075630938351134)
XLA Ops:
  0.7 1.5 %multiply_bitcast_fusion = f32[1,16,8192]{2,1,0:T(8,128)S(1)} fusion(f32[16,8192]{1,0:T(8,128)} %param.19, f32[16,8192]{1,0:T(8,128)} %param.18), kind=kLoop, calls=%fused_computation.125 | loop fusion | flops 131072 | bytes 1572864 | tf_op jit(solution)/shard_map/stack | solution.py:91
  2.2 2.0 %pad_maximum_fusion.18 = (f32[3,1,8192]{2,1,0:T(1,128)}, f32[3,1,8192]{2,1,0:T(1,128)}) fusion(f32[1,16,8192]{2,1,0:T(8,128)} %bitcast.50, f32[1,16,8192]{2,1,0:T(8,128)S(1)} %multiply_bitcast_fusion, f32[1,16,8192]{2,1,0:T(8,128)} %bitcast.42), kind=kLoop, calls=%fused_computation.144 | loop fusion | flops 98304 | bytes 1769472 | tf_op jit(solution)/shard_map/slice | solution.py:17
  4.2 5.2 %collective-permute-start.4 = (f32[3,1,8192]{2,1,0:T(1,128)}, f32[3,1,8192]{2,1,0:T(1,128)}, u32[]{:S(2)}, u32[]{:S(2)}) collective-permute-start(f32[3,1,8192]{2,1,0:T(1,128)} %get-tuple-element.35), channel_id=1, source_target_pairs={{0,16},{16,32},{32,48},{48,64},{64,80},{80,96},{96,112},{112,128},... | collective-permute-start | bytes 294920 | tf_op jit(solution)/shard_map/ppermute | solution.py:20
  9.4 4.0 %collective-permute-start.5 = (f32[3,1,8192]{2,1,0:T(1,128)}, f32[3,1,8192]{2,1,0:T(1,128)}, u32[]{:S(2)}, u32[]{:S(2)}) collective-permute-start(f32[3,1,8192]{2,1,0:T(1,128)} %get-tuple-element.36), channel_id=1, source_target_pairs={{16,0},{32,16},{48,32},{64,48},{80,64},{96,80},{112,96},{128,112},... | collective-permute-start | bytes 294920 | tf_op jit(solution)/shard_map/ppermute | solution.py:22
  13.5 0.1 pad_maximum_fusion.20
  13.6 3.4 %collective-permute-start = (f32[2,16,1,512]{3,2,1,0:T(1,128)S(1)}, f32[2,16,1,512]{3,2,1,0:T(1,128)S(1)}, u32[]{:S(2)}, u32[]{:S(2)}) collective-permute-start(f32[2,16,1,512]{3,2,1,0:T(1,128)S(1)} %get-tuple-element.39), channel_id=1, source_target_pairs={{0,16},{16,32},{32,48},{48,64},{64,80},{80,96},{96,112},{112,128},... | collective-permute-start | bytes 196616 | tf_op jit(solution)/shard_map/ppermute | solution.py:20
  17.0 5.5 %collective-permute-start.1 = (f32[2,16,1,512]{3,2,1,0:T(1,128)S(1)}, f32[2,16,1,512]{3,2,1,0:T(1,128)S(1)}, u32[]{:S(2)}, u32[]{:S(2)}) collective-permute-start(f32[2,16,1,512]{3,2,1,0:T(1,128)S(1)} %get-tuple-element.40), channel_id=1, source_target_pairs={{16,0},{32,16},{48,32},{64,48},{80,64},{96,80},{112,96},{128,112},... | collective-permute-start | bytes 196616 | tf_op jit(solution)/shard_map/ppermute | solution.py:22
  22.5 0.1 select_reduce_fusion
  22.6 0.1 divide_subtract_fusion
  22.7 0.0 collective-permute-done
  22.8 2.6 %collective-permute-done.1 = f32[2,16,1,512]{3,2,1,0:T(1,128)S(1)} collective-permute-done((f32[2,16,1,512]{3,2,1,0:T(1,128)S(1)}, f32[2,16,1,512]{3,2,1,0:T(1,128)S(1)}, u32[]{:S(2)}, u32[]{:S(2)}) %collective-permute-start.1) | collective-permute-done | bytes 65568 | tf_op jit(solution)/shard_map/ppermute | solution.py:22
  25.3 0.2 pad_maximum_fusion.12
  25.6 1.9 %collective-permute-start.2 = (f32[2,16,18,1]{3,2,1,0:T(8,128)S(1)}, f32[2,16,18,1]{3,2,1,0:T(8,128)}, u32[]{:S(2)}, u32[]{:S(2)}) collective-permute-start(f32[2,16,18,1]{3,2,1,0:T(8,128)S(1)} %get-tuple-element.37), channel_id=1, source_target_pairs={{0,1},{1,2},{2,3},{3,4},{4,5},{5,6},{6,7},{7,8},{8,9},{9,10},{10,1... | collective-permute-start | bytes 6920 | tf_op jit(solution)/shard_map/ppermute | solution.py:20
  27.5 4.7 %collective-permute-start.3 = (f32[2,16,18,1]{3,2,1,0:T(8,128)S(1)}, f32[2,16,18,1]{3,2,1,0:T(8,128)}, u32[]{:S(2)}, u32[]{:S(2)}) collective-permute-start(f32[2,16,18,1]{3,2,1,0:T(8,128)S(1)} %get-tuple-element.38), channel_id=1, source_target_pairs={{1,0},{2,1},{3,2},{4,3},{5,4},{6,5},{7,6},{8,7},{9,8},{10,9},{11,1... | collective-permute-start | bytes 6920 | tf_op jit(solution)/shard_map/ppermute | solution.py:22
  32.2 41.6 %all-gather = f32[1,16,8192]{2,1,0:T(8,128)S(1)} all-gather(f32[1,16,512]{2,1,0:T(8,128)S(1)} %slice.287), channel_id=2, replica_groups=mesh['gx'=16,'gy'=8,'ga'=2] {'gy','ga'}, dimensions={2}, use_global_device_ids=true | all-gather | bytes 557056 | tf_op jit(solution)/shard_map/all_gather | solution.py:87
  73.8 0.0 collective-permute-done.2
  73.8 0.0 collective-permute-done.3
  73.8 2.3 %pad_maximum_fusion = f32[2,16,18,514]{3,2,1,0:T(8,128)S(1)} fusion(f32[2,16,18,1]{3,2,1,0:T(8,128)} %collective-permute-done.3, f32[2,16,1,512]{3,2,1,0:T(1,128)S(1)} %collective-permute-done.1, f32[1,16,16,512]{3,2,1,0:T(8,128)S(1)} %bitcast.49, f32[1,16,16,512]{3,2,1,0:T(8,128)S(1)} %bitcast.46, f32[2,16,1,512]{3,2,1,0:T(1,128)S(1)} %collective-permute-done, ...), kind=kLoop, calls=%fused_computation.7 | loop fusion | flops 1480320 | bytes 2368512 | tf_op jit(solution)/shard_map/concatenate | solution.py:18
  76.1 0.0 copy-start
  76.1 0.0 copy-start.4
  76.1 0.1 slice_bitcast_fusion.1
  76.3 0.0 collective-permute-done.4
  76.3 0.0 collective-permute-done.5
  76.3 0.9 copy-done
  77.1 0.2 copy-done.4
  77.3 2.0 %select_maximum_fusion = f32[3,18,8194]{2,1,0:T(8,128)S(1)} fusion(f32[3,1,8192]{2,1,0:T(1,128)} %collective-permute-done.5, f32[3,1,8192]{2,1,0:T(1,128)} %collective-permute-done.4, f32[1,16,8192]{2,1,0:T(8,128)S(1)} %bitcast.51, f32[1,16,8192]{2,1,0:T(8,128)S(1)} %multiply_bitcast_fusion, f32[1,16,8192]{2,1,0:T(8,128)S(1)} %bitcast.43), kind=kLoop, calls=%fused_computation.2 | loop fusion | flops 5309712 | bytes 3539376 | tf_op jit(solution)/shard_map/concatenate | solution.py:18
  79.3 0.0 copy-start.2
  79.4 0.1 slice_bitcast_fusion.4
  79.5 0.1 fusion.4
  79.6 0.8 copy-done.2
  80.4 1.3 fusion.59
  81.8 7.0 %collective-permute-start.6 = (f32[1,8192]{1,0:T(1,128)S(1)}, f32[1,8192]{1,0:T(1,128)S(1)}, u32[]{:S(2)}, u32[]{:S(2)}) collective-permute-start(f32[1,8192]{1,0:T(1,128)S(1)} %get-tuple-element.54), channel_id=1, source_target_pairs={{0,16},{16,32},{32,48},{48,64},{64,80},{80,96},{96,112},{112,128},... | collective-permute-start | bytes 98312 | tf_op jit(solution)/shard_map/ppermute | solution.py:20
  88.7 1.9 %collective-permute-start.7 = (f32[1,8192]{1,0:T(1,128)S(1)}, f32[1,8192]{1,0:T(1,128)S(1)}, u32[]{:S(2)}, u32[]{:S(2)}) collective-permute-start(f32[1,8192]{1,0:T(1,128)S(1)} %get-tuple-element.55), channel_id=1, source_target_pairs={{16,0},{32,16},{48,32},{64,48},{80,64},{96,80},{112,96},{128,112},... | collective-permute-start | bytes 98312 | tf_op jit(solution)/shard_map/ppermute | solution.py:22
  90.7 0.3 fusion.69
  91.0 0.0 collective-permute-done.6
  91.0 4.4 %collective-permute-done.7 = f32[1,8192]{1,0:T(1,128)S(1)} collective-permute-done((f32[1,8192]{1,0:T(1,128)S(1)}, f32[1,8192]{1,0:T(1,128)S(1)}, u32[]{:S(2)}, u32[]{:S(2)}) %collective-permute-start.7) | collective-permute-done | bytes 32800 | tf_op jit(solution)/shard_map/ppermute | solution.py:22
  95.4 0.4 fusion.3
  95.9 0.8 fusion.52
  96.7 3.1 %collective-permute-start.8 = (f32[1,8192]{1,0:T(1,128)S(1)}, f32[1,8192]{1,0:T(1,128)S(1)}, u32[]{:S(2)}, u32[]{:S(2)}) collective-permute-start(f32[1,8192]{1,0:T(1,128)S(1)} %get-tuple-element.52), channel_id=1, source_target_pairs={{0,16},{16,32},{32,48},{48,64},{64,80},{80,96},{96,112},{112,128},... | collective-permute-start | bytes 98312 | tf_op jit(solution)/shard_map/ppermute | solution.py:20
  99.9 5.7 %collective-permute-start.9 = (f32[1,8192]{1,0:T(1,128)S(1)}, f32[1,8192]{1,0:T(1,128)S(1)}, u32[]{:S(2)}, u32[]{:S(2)}) collective-permute-start(f32[1,8192]{1,0:T(1,128)S(1)} %get-tuple-element.53), channel_id=1, source_target_pairs={{16,0},{32,16},{48,32},{64,48},{80,64},{96,80},{112,96},{128,112},... | collective-permute-start | bytes 98312 | tf_op jit(solution)/shard_map/ppermute | solution.py:22
  105.6 0.3 fusion.63
  105.9 0.0 collective-permute-done.8
  105.9 1.2 collective-permute-done.9
  107.2 0.4 fusion.2
  107.6 0.8 fusion.45
  108.4 4.1 %collective-permute-start.10 = (f32[1,8192]{1,0:T(1,128)S(1)}, f32[1,8192]{1,0:T(1,128)S(1)}, u32[]{:S(2)}, u32[]{:S(2)}) collective-permute-start(f32[1,8192]{1,0:T(1,128)S(1)} %get-tuple-element.50), channel_id=1, source_target_pairs={{0,16},{16,32},{32,48},{48,64},{64,80},{80,96},{96,112},{112,128},... | collective-permute-start | bytes 98312 | tf_op jit(solution)/shard_map/ppermute | solution.py:20
  112.5 5.1 %collective-permute-start.11 = (f32[1,8192]{1,0:T(1,128)S(1)}, f32[1,8192]{1,0:T(1,128)S(1)}, u32[]{:S(2)}, u32[]{:S(2)}) collective-permute-start(f32[1,8192]{1,0:T(1,128)S(1)} %get-tuple-element.51), channel_id=1, source_target_pairs={{16,0},{32,16},{48,32},{64,48},{80,64},{96,80},{112,96},{128,112},... | collective-permute-start | bytes 98312 | tf_op jit(solution)/shard_map/ppermute | solution.py:22
  117.6 1.6 %collective-permute-done.11 = f32[1,8192]{1,0:T(1,128)S(1)} collective-permute-done((f32[1,8192]{1,0:T(1,128)S(1)}, f32[1,8192]{1,0:T(1,128)S(1)}, u32[]{:S(2)}, u32[]{:S(2)}) %collective-permute-start.11) | collective-permute-done | bytes 32800 | tf_op jit(solution)/shard_map/ppermute | solution.py:22
  119.2 0.4 fusion.1
  119.6 0.8 fusion.38
  120.4 0.0 copy-start.5
  120.5 1.4 fusion.31
  121.9 0.1 fusion.71
  121.9 7.2 %collective-permute-start.12 = (f32[16,1,512]{2,1,0:T(1,128)S(1)}, f32[16,1,512]{2,1,0:T(1,128)S(1)}, u32[]{:S(2)}, u32[]{:S(2)}) collective-permute-start(f32[16,1,512]{2,1,0:T(1,128)S(1)} %get-tuple-element.48), channel_id=1, source_target_pairs={{16,0},{32,16},{48,32},{64,48},{80,64},{96,80},{112,96},{128,112},... | collective-permute-start | bytes 98312 | tf_op jit(solution)/shard_map/ppermute | solution.py:22
  129.2 1.9 %collective-permute-start.13 = (f32[16,1,512]{2,1,0:T(1,128)S(1)}, f32[16,1,512]{2,1,0:T(1,128)S(1)}, u32[]{:S(2)}, u32[]{:S(2)}) collective-permute-start(f32[16,1,512]{2,1,0:T(1,128)S(1)} %get-tuple-element.47), channel_id=1, source_target_pairs={{0,16},{16,32},{32,48},{48,64},{64,80},{80,96},{96,112},{112,128},... | collective-permute-start | bytes 98312 | tf_op jit(solution)/shard_map/ppermute | solution.py:20
  131.1 0.0 collective-permute-done.12
  131.1 7.0 %collective-permute-done.13 = f32[16,1,512]{2,1,0:T(1,128)S(1)} collective-permute-done((f32[16,1,512]{2,1,0:T(1,128)S(1)}, f32[16,1,512]{2,1,0:T(1,128)S(1)}, u32[]{:S(2)}, u32[]{:S(2)}) %collective-permute-start.13) | collective-permute-done | bytes 32800 | tf_op jit(solution)/shard_map/ppermute | solution.py:20
  138.1 0.2 pad_maximum_fusion.15
  138.3 1.9 %collective-permute-start.14 = (f32[16,18,1]{2,1,0:T(8,128)S(1)}, f32[16,18,1]{2,1,0:T(8,128)S(1)}, u32[]{:S(2)}, u32[]{:S(2)}) collective-permute-start(f32[16,18,1]{2,1,0:T(8,128)S(1)} %get-tuple-element.43), channel_id=1, source_target_pairs={{1,0},{2,1},{3,2},{4,3},{5,4},{6,5},{7,6},{8,7},{9,8},{10,9},{11,1... | collective-permute-start | bytes 3464 | tf_op jit(solution)/shard_map/ppermute | solution.py:22
  140.2 3.6 %collective-permute-start.15 = (f32[16,18,1]{2,1,0:T(8,128)S(1)}, f32[16,18,1]{2,1,0:T(8,128)S(1)}, u32[]{:S(2)}, u32[]{:S(2)}) collective-permute-start(f32[16,18,1]{2,1,0:T(8,128)S(1)} %get-tuple-element.44), channel_id=1, source_target_pairs={{0,1},{1,2},{2,3},{3,4},{4,5},{5,6},{6,7},{7,8},{8,9},{9,10},{10,1... | collective-permute-start | bytes 3464 | tf_op jit(solution)/shard_map/ppermute | solution.py:20
  143.8 0.1 fusion.70
  144.0 1.3 collective-permute-done.14
  145.3 4.2 %collective-permute-done.15 = f32[16,18,1]{2,1,0:T(8,128)S(1)} collective-permute-done((f32[16,18,1]{2,1,0:T(8,128)S(1)}, f32[16,18,1]{2,1,0:T(8,128)S(1)}, u32[]{:S(2)}, u32[]{:S(2)}) %collective-permute-start.15) | collective-permute-done | bytes 1184 | tf_op jit(solution)/shard_map/ppermute | solution.py:20
  149.5 2.3 %fusion.20 = f32[16,16,512]{2,1,0:T(8,128)} fusion(f32[16,16,512]{2,1,0:T(8,128)S(1)} %fusion.64, f32[16,18,1]{2,1,0:T(8,128)S(1)} %collective-permute-done.15, f32[16,1,512]{2,1,0:T(1,128)S(1)} %collective-permute-done.12, f32[16,16,512]{2,1,0:T(8,128)S(1)} %fusion.31, f32[16,1,512]{2,1,0:T(1,128)S(1)} %collective-permute-done.13, ...), kind=kLoop, calls=%fused_computation.52 | loop fusion | flops 6946816 | bytes 5769472 | tf_op jit(solution)/shard_map/jit(_where)/select_n | solution.py:51
  (19 shorter events, 0.2 us)
Async XLA Ops:
  0.6 12.8 %copy-start.1 = (f32[16,16,512]{2,1,0:T(8,128)S(1)}, f32[16,16,512]{2,1,0:T(8,128)}, u32[]{:S(2)}) copy-start(f32[16,16,512]{2,1,0:T(8,128)} %param.13) | copy-start | bytes 1572868
  0.6 12.8 %copy-start.3 = (f32[16,16,512]{2,1,0:T(8,128)S(1)}, f32[16,16,512]{2,1,0:T(8,128)}, u32[]{:S(2)}) copy-start(f32[16,16,512]{2,1,0:T(8,128)} %param.14) | copy-start | bytes 1572868
  0.7 21.8 %copy-start.6 = (s32[16,512]{1,0:T(8,128)S(1)}, s32[16,512]{1,0:T(8,128)}, u32[]{:S(2)}) copy-start(s32[16,512]{1,0:T(8,128)} %param.15) | copy-start | bytes 98308
  0.7 21.8 %copy-start.7 = (s32[16,512]{1,0:T(8,128)S(1)}, s32[16,512]{1,0:T(8,128)}, u32[]{:S(2)}) copy-start(s32[16,512]{1,0:T(8,128)} %param.16) | copy-start | bytes 98308
  0.7 21.8 %copy-start.8 = (f32[17]{0:T(128)S(1)}, f32[17]{0:T(128)}, u32[]{:S(2)}) copy-start(f32[17]{0:T(128)} %param.17) | copy-start | bytes 208
  4.2 72.0 %collective-permute-start.4 = (f32[3,1,8192]{2,1,0:T(1,128)}, f32[3,1,8192]{2,1,0:T(1,128)}, u32[]{:S(2)}, u32[]{:S(2)}) collective-permute-start(f32[3,1,8192]{2,1,0:T(1,128)} %get-tuple-element.35), channel_id=1, source_target_pairs={{0,16},{16,32},{32,48},{48,64},{64,80},{80,96},{96,112},{112,128},... | collective-permute-start | bytes 294920 | tf_op jit(solution)/shard_map/ppermute | solution.py:20
  9.4 66.9 %collective-permute-start.5 = (f32[3,1,8192]{2,1,0:T(1,128)}, f32[3,1,8192]{2,1,0:T(1,128)}, u32[]{:S(2)}, u32[]{:S(2)}) collective-permute-start(f32[3,1,8192]{2,1,0:T(1,128)} %get-tuple-element.36), channel_id=1, source_target_pairs={{16,0},{32,16},{48,32},{64,48},{80,64},{96,80},{112,96},{128,112},... | collective-permute-start | bytes 294920 | tf_op jit(solution)/shard_map/ppermute | solution.py:22
  13.6 9.2 %collective-permute-start = (f32[2,16,1,512]{3,2,1,0:T(1,128)S(1)}, f32[2,16,1,512]{3,2,1,0:T(1,128)S(1)}, u32[]{:S(2)}, u32[]{:S(2)}) collective-permute-start(f32[2,16,1,512]{3,2,1,0:T(1,128)S(1)} %get-tuple-element.39), channel_id=1, source_target_pairs={{0,16},{16,32},{32,48},{48,64},{64,80},{80,96},{96,112},{112,128},... | collective-permute-start | bytes 196616 | tf_op jit(solution)/shard_map/ppermute | solution.py:20
  17.0 8.4 %collective-permute-start.1 = (f32[2,16,1,512]{3,2,1,0:T(1,128)S(1)}, f32[2,16,1,512]{3,2,1,0:T(1,128)S(1)}, u32[]{:S(2)}, u32[]{:S(2)}) collective-permute-start(f32[2,16,1,512]{3,2,1,0:T(1,128)S(1)} %get-tuple-element.40), channel_id=1, source_target_pairs={{16,0},{32,16},{48,32},{64,48},{80,64},{96,80},{112,96},{128,112},... | collective-permute-start | bytes 196616 | tf_op jit(solution)/shard_map/ppermute | solution.py:22
  25.6 48.2 %collective-permute-start.2 = (f32[2,16,18,1]{3,2,1,0:T(8,128)S(1)}, f32[2,16,18,1]{3,2,1,0:T(8,128)}, u32[]{:S(2)}, u32[]{:S(2)}) collective-permute-start(f32[2,16,18,1]{3,2,1,0:T(8,128)S(1)} %get-tuple-element.37), channel_id=1, source_target_pairs={{0,1},{1,2},{2,3},{3,4},{4,5},{5,6},{6,7},{7,8},{8,9},{9,10},{10,1... | collective-permute-start | bytes 6920 | tf_op jit(solution)/shard_map/ppermute | solution.py:20
  27.5 46.3 %collective-permute-start.3 = (f32[2,16,18,1]{3,2,1,0:T(8,128)S(1)}, f32[2,16,18,1]{3,2,1,0:T(8,128)}, u32[]{:S(2)}, u32[]{:S(2)}) collective-permute-start(f32[2,16,18,1]{3,2,1,0:T(8,128)S(1)} %get-tuple-element.38), channel_id=1, source_target_pairs={{1,0},{2,1},{3,2},{4,3},{5,4},{6,5},{7,6},{8,7},{9,8},{10,9},{11,1... | collective-permute-start | bytes 6920 | tf_op jit(solution)/shard_map/ppermute | solution.py:22
  76.1 1.0 copy-start
  76.1 1.2 copy-start.4
  79.3 1.0 copy-start.2
  81.8 9.2 %collective-permute-start.6 = (f32[1,8192]{1,0:T(1,128)S(1)}, f32[1,8192]{1,0:T(1,128)S(1)}, u32[]{:S(2)}, u32[]{:S(2)}) collective-permute-start(f32[1,8192]{1,0:T(1,128)S(1)} %get-tuple-element.54), channel_id=1, source_target_pairs={{0,16},{16,32},{32,48},{48,64},{64,80},{80,96},{96,112},{112,128},... | collective-permute-start | bytes 98312 | tf_op jit(solution)/shard_map/ppermute | solution.py:20
  88.7 6.7 %collective-permute-start.7 = (f32[1,8192]{1,0:T(1,128)S(1)}, f32[1,8192]{1,0:T(1,128)S(1)}, u32[]{:S(2)}, u32[]{:S(2)}) collective-permute-start(f32[1,8192]{1,0:T(1,128)S(1)} %get-tuple-element.55), channel_id=1, source_target_pairs={{16,0},{32,16},{48,32},{64,48},{80,64},{96,80},{112,96},{128,112},... | collective-permute-start | bytes 98312 | tf_op jit(solution)/shard_map/ppermute | solution.py:22
  96.7 9.2 %collective-permute-start.8 = (f32[1,8192]{1,0:T(1,128)S(1)}, f32[1,8192]{1,0:T(1,128)S(1)}, u32[]{:S(2)}, u32[]{:S(2)}) collective-permute-start(f32[1,8192]{1,0:T(1,128)S(1)} %get-tuple-element.52), channel_id=1, source_target_pairs={{0,16},{16,32},{32,48},{48,64},{64,80},{80,96},{96,112},{112,128},... | collective-permute-start | bytes 98312 | tf_op jit(solution)/shard_map/ppermute | solution.py:20
  99.9 7.3 %collective-permute-start.9 = (f32[1,8192]{1,0:T(1,128)S(1)}, f32[1,8192]{1,0:T(1,128)S(1)}, u32[]{:S(2)}, u32[]{:S(2)}) collective-permute-start(f32[1,8192]{1,0:T(1,128)S(1)} %get-tuple-element.53), channel_id=1, source_target_pairs={{16,0},{32,16},{48,32},{64,48},{80,64},{96,80},{112,96},{128,112},... | collective-permute-start | bytes 98312 | tf_op jit(solution)/shard_map/ppermute | solution.py:22
  108.4 9.2 %collective-permute-start.10 = (f32[1,8192]{1,0:T(1,128)S(1)}, f32[1,8192]{1,0:T(1,128)S(1)}, u32[]{:S(2)}, u32[]{:S(2)}) collective-permute-start(f32[1,8192]{1,0:T(1,128)S(1)} %get-tuple-element.50), channel_id=1, source_target_pairs={{0,16},{16,32},{32,48},{48,64},{64,80},{80,96},{96,112},{112,128},... | collective-permute-start | bytes 98312 | tf_op jit(solution)/shard_map/ppermute | solution.py:20
  112.5 6.7 %collective-permute-start.11 = (f32[1,8192]{1,0:T(1,128)S(1)}, f32[1,8192]{1,0:T(1,128)S(1)}, u32[]{:S(2)}, u32[]{:S(2)}) collective-permute-start(f32[1,8192]{1,0:T(1,128)S(1)} %get-tuple-element.51), channel_id=1, source_target_pairs={{16,0},{32,16},{48,32},{64,48},{80,64},{96,80},{112,96},{128,112},... | collective-permute-start | bytes 98312 | tf_op jit(solution)/shard_map/ppermute | solution.py:22
  120.4 1.5 copy-start.5
  121.9 9.2 %collective-permute-start.12 = (f32[16,1,512]{2,1,0:T(1,128)S(1)}, f32[16,1,512]{2,1,0:T(1,128)S(1)}, u32[]{:S(2)}, u32[]{:S(2)}) collective-permute-start(f32[16,1,512]{2,1,0:T(1,128)S(1)} %get-tuple-element.48), channel_id=1, source_target_pairs={{16,0},{32,16},{48,32},{64,48},{80,64},{96,80},{112,96},{128,112},... | collective-permute-start | bytes 98312 | tf_op jit(solution)/shard_map/ppermute | solution.py:22
  129.2 8.9 %collective-permute-start.13 = (f32[16,1,512]{2,1,0:T(1,128)S(1)}, f32[16,1,512]{2,1,0:T(1,128)S(1)}, u32[]{:S(2)}, u32[]{:S(2)}) collective-permute-start(f32[16,1,512]{2,1,0:T(1,128)S(1)} %get-tuple-element.47), channel_id=1, source_target_pairs={{0,16},{16,32},{32,48},{48,64},{64,80},{80,96},{96,112},{112,128},... | collective-permute-start | bytes 98312 | tf_op jit(solution)/shard_map/ppermute | solution.py:20
  138.3 7.0 %collective-permute-start.14 = (f32[16,18,1]{2,1,0:T(8,128)S(1)}, f32[16,18,1]{2,1,0:T(8,128)S(1)}, u32[]{:S(2)}, u32[]{:S(2)}) collective-permute-start(f32[16,18,1]{2,1,0:T(8,128)S(1)} %get-tuple-element.43), channel_id=1, source_target_pairs={{1,0},{2,1},{3,2},{4,3},{5,4},{6,5},{7,6},{8,7},{9,8},{10,9},{11,1... | collective-permute-start | bytes 3464 | tf_op jit(solution)/shard_map/ppermute | solution.py:22
  140.2 9.3 %collective-permute-start.15 = (f32[16,18,1]{2,1,0:T(8,128)S(1)}, f32[16,18,1]{2,1,0:T(8,128)S(1)}, u32[]{:S(2)}, u32[]{:S(2)}) collective-permute-start(f32[16,18,1]{2,1,0:T(8,128)S(1)} %get-tuple-element.44), channel_id=1, source_target_pairs={{0,1},{1,2},{2,3},{3,4},{4,5},{5,6},{6,7},{7,8},{8,9},{9,10},{10,1... | collective-permute-start | bytes 3464 | tf_op jit(solution)/shard_map/ppermute | solution.py:20
where the time goes:
time: 152 us
  starting transfers between devices  66.2 us (44%)
  blocking collectives  41.6 us (27%)
  waiting for transfers between devices  22.3 us (15%)
  other arithmetic  17.7 us (12%)
  local copies, waits for them, and re-layouts  2.78 us (2%)
    all_gather x1, blocking collectives, body(): top_rows = lax.all_gather(top, ('gy', 'ga'), axis=1, tiled=True)  41.6 us
    ppermute x8, starting transfers between devices, with_halo(): lax.ppermute(head, axis, [((i + 1) % count, i) for i in range(ends)])  36 us
    ppermute x8, starting transfers between devices, with_halo(): lax.ppermute(tail, axis, [(i, (i + 1) % count) for i in range(ends)])  30.2 us
    ppermute x8, waiting for transfers between devices, with_halo(): lax.ppermute(tail, axis, [(i, (i + 1) % count) for i in range(ends)])  11.2 us
    ppermute x8, waiting for transfers between devices, with_halo(): lax.ppermute(head, axis, [((i + 1) % count, i) for i in range(ends)])  11.1 us
    select_n x6, other arithmetic, guarded(): return jnp.where(denom > 0, numer / jnp.where(denom > 0, denom, 1.0), 0.0)  7.39 us
    concatenate x2, other arithmetic, with_halo(): jnp.concatenate([lax.ppermute(tail, axis, [(i, (i + 1) % count) for i in...  4.3 us
  transfers between devices with their start and end apart: 16, of which 7 were waited for; matrix products, arithmetic and copies ran while one was open for 2% of the time, Pallas kernels for 0%

commit v1 on v0

--- a/solution.py
+++ b/solution.py
@@ -84,7 +84,13 @@
     coupling_rows = exchange_coef * land_mask.astype(jnp.float32)
     coupling = lax.dynamic_slice_in_dim(coupling_rows, offset, cols_here, 1)
     top = head[0]
-    top_rows = lax.all_gather(top, ("gy", "ga"), axis=1, tiled=True)
+
+    def trees_supply_all(x_local, mesh_ax):
+        return jnp.concatenate(
+            lax.all_to_all(jnp.stack(lax.axis_size(mesh_ax) * [x_local]), mesh_ax, 0, 0), axis=1
+        )
+
+    top_rows = trees_supply_all(top, ("gy", "ga"))
     drag = conveyance * jnp.power(depth, 5.0 / 3.0)
     sbase = depth + coupling_rows * top_rows
     sdiag = 1.0 + coupling_rows

time: 152 us -> 137 us (0.901)
  the two profiles are of different devices: /device:TPU:34 before, /device:TPU:47 now
where the time goes in v1:
time: 137 us; the launch traced here: 136 us
  starting transfers between devices  75.1 us (55%)
  waiting for transfers between devices  32.9 us (24%)
  other arithmetic  20.1 us (15%)
  local copies, waits for them, and re-layouts  6.75 us (5%)
    ppermute x8, starting transfers between devices, with_halo(): lax.ppermute(head, axis, [((i + 1) % count, i) for i in range(ends)])  35.1 us
    ppermute x8, starting transfers between devices, with_halo(): lax.ppermute(tail, axis, [(i, (i + 1) % count) for i in range(ends)])  33.6 us
    ppermute x8, waiting for transfers between devices, with_halo(): lax.ppermute(head, axis, [((i + 1) % count, i) for i in range(ends)])  17.8 us
    ppermute x8, waiting for transfers between devices, with_halo(): lax.ppermute(tail, axis, [(i, (i + 1) % count) for i in range(ends)])  15.1 us
    select_n x6, other arithmetic, guarded(): return jnp.where(denom > 0, numer / jnp.where(denom > 0, denom, 1.0), 0.0)  9.99 us
    all_to_all x1, starting transfers between devices, trees_supply_all(): lax.all_to_all(jnp.stack(lax.axis_size(mesh_ax) * [x_local]), mesh_ax, 0, 0)  6.39 us
    concatenate x2, other arithmetic, with_halo(): jnp.concatenate([lax.ppermute(tail, axis, [(i, (i + 1) % count) for i in...  3.15 us
  transfers between devices with their start and end apart: 17, of which 9 were waited for; matrix products, arithmetic and copies ran while one was open for 7% of the time, Pallas kernels for 0%

profile of v1, /device:TPU:47, one launch (start us, length us, event | category | flops | bytes accessed | tf_op | source)
XLA Modules:
  0.0 136.0 jit_solution(1927663944034928425)
XLA Ops:
  0.6 1.6 %multiply_bitcast_fusion = f32[1,16,8192]{2,1,0:T(8,128)S(1)} fusion(f32[16,8192]{1,0:T(8,128)} %param.19, f32[16,8192]{1,0:T(8,128)} %param.18), kind=kLoop, calls=%fused_computation.124 | loop fusion | flops 131072 | bytes 1572864 | tf_op jit(solution)/shard_map/stack | solution.py:97
  2.2 0.0 copy-start.8
  2.2 0.0 copy-start.13
  2.2 0.0 copy-start.14
  2.3 0.7 copy-done.8
  3.0 1.3 pad_maximum_fusion.18
  4.3 4.9 %collective-permute-start.4 = (f32[3,1,8192]{2,1,0:T(1,128)S(1)}, f32[3,1,8192]{2,1,0:T(1,128)S(1)}, u32[]{:S(2)}, u32[]{:S(2)}) collective-permute-start(f32[3,1,8192]{2,1,0:T(1,128)S(1)} %get-tuple-element.35), channel_id=1, source_target_pairs={{0,16},{16,32},{32,48},{48,64},{64,80},{80,96},{96,112},{112,128},... | collective-permute-start | bytes 294920 | tf_op jit(solution)/shard_map/ppermute | solution.py:20
  9.2 4.3 %collective-permute-start.5 = (f32[3,1,8192]{2,1,0:T(1,128)S(1)}, f32[3,1,8192]{2,1,0:T(1,128)}, u32[]{:S(2)}, u32[]{:S(2)}) collective-permute-start(f32[3,1,8192]{2,1,0:T(1,128)S(1)} %get-tuple-element.36), channel_id=1, source_target_pairs={{16,0},{32,16},{48,32},{64,48},{80,64},{96,80},{112,96},{128,112},... | collective-permute-start | bytes 294920 | tf_op jit(solution)/shard_map/ppermute | solution.py:22
  13.6 0.9 stack.31
  14.4 6.4 %all-to-all-start = ((f32[16,16,512]{2,1,0:T(8,128)}), f32[16,16,512]{2,1,0:T(8,128)}, u32[]{:S(2)}, u32[]{:S(2)}) async-start(f32[16,16,512]{2,1,0:T(8,128)} %stack.31), calls=%async_computation | async-start | bytes 1048576 | tf_op jit(solution)/shard_map/all_to_all | solution.py:90
  20.8 0.1 pad_maximum_fusion.20
  21.0 2.8 %collective-permute-start = (f32[2,16,1,512]{3,2,1,0:T(1,128)S(1)}, f32[2,16,1,512]{3,2,1,0:T(1,128)S(1)}, u32[]{:S(2)}, u32[]{:S(2)}) collective-permute-start(f32[2,16,1,512]{3,2,1,0:T(1,128)S(1)} %get-tuple-element.39), channel_id=1, source_target_pairs={{0,16},{16,32},{32,48},{48,64},{64,80},{80,96},{96,112},{112,128},... | collective-permute-start | bytes 196616 | tf_op jit(solution)/shard_map/ppermute | solution.py:20
  23.8 5.5 %collective-permute-start.1 = (f32[2,16,1,512]{3,2,1,0:T(1,128)S(1)}, f32[2,16,1,512]{3,2,1,0:T(1,128)S(1)}, u32[]{:S(2)}, u32[]{:S(2)}) collective-permute-start(f32[2,16,1,512]{3,2,1,0:T(1,128)S(1)} %get-tuple-element.40), channel_id=1, source_target_pairs={{16,0},{32,16},{48,32},{64,48},{80,64},{96,80},{112,96},{128,112},... | collective-permute-start | bytes 196616 | tf_op jit(solution)/shard_map/ppermute | solution.py:22
  29.3 0.1 select_reduce_fusion
  29.4 1.8 %collective-permute-done.1 = f32[2,16,1,512]{3,2,1,0:T(1,128)S(1)} collective-permute-done((f32[2,16,1,512]{3,2,1,0:T(1,128)S(1)}, f32[2,16,1,512]{3,2,1,0:T(1,128)S(1)}, u32[]{:S(2)}, u32[]{:S(2)}) %collective-permute-start.1) | collective-permute-done | bytes 65568 | tf_op jit(solution)/shard_map/ppermute | solution.py:22
  31.3 0.2 pad_maximum_fusion.12
  31.5 5.9 %collective-permute-start.2 = (f32[2,16,18,1]{3,2,1,0:T(8,128)S(1)}, f32[2,16,18,1]{3,2,1,0:T(8,128)S(1)}, u32[]{:S(2)}, u32[]{:S(2)}) collective-permute-start(f32[2,16,18,1]{3,2,1,0:T(8,128)S(1)} %get-tuple-element.37), channel_id=1, source_target_pairs={{0,1},{1,2},{2,3},{3,4},{4,5},{5,6},{6,7},{7,8},{8,9},{9,10},{10,1... | collective-permute-start | bytes 6920 | tf_op jit(solution)/shard_map/ppermute | solution.py:20
  37.5 1.9 %collective-permute-start.3 = (f32[2,16,18,1]{3,2,1,0:T(8,128)S(1)}, f32[2,16,18,1]{3,2,1,0:T(8,128)S(1)}, u32[]{:S(2)}, u32[]{:S(2)}) collective-permute-start(f32[2,16,18,1]{3,2,1,0:T(8,128)S(1)} %get-tuple-element.38), channel_id=1, source_target_pairs={{1,0},{2,1},{3,2},{4,3},{5,4},{6,5},{7,6},{8,7},{9,8},{10,9},{11,1... | collective-permute-start | bytes 6920 | tf_op jit(solution)/shard_map/ppermute | solution.py:22
  39.4 0.9 divide_subtract_fusion
  40.3 6.1 %collective-permute-done.2 = f32[2,16,18,1]{3,2,1,0:T(8,128)S(1)} collective-permute-done((f32[2,16,18,1]{3,2,1,0:T(8,128)S(1)}, f32[2,16,18,1]{3,2,1,0:T(8,128)S(1)}, u32[]{:S(2)}, u32[]{:S(2)}) %collective-permute-start.2) | collective-permute-done | bytes 2336 | tf_op jit(solution)/shard_map/ppermute | solution.py:20
  46.4 7.5 %collective-permute-done.3 = f32[2,16,18,1]{3,2,1,0:T(8,128)S(1)} collective-permute-done((f32[2,16,18,1]{3,2,1,0:T(8,128)S(1)}, f32[2,16,18,1]{3,2,1,0:T(8,128)S(1)}, u32[]{:S(2)}, u32[]{:S(2)}) %collective-permute-start.3) | collective-permute-done | bytes 2336 | tf_op jit(solution)/shard_map/ppermute | solution.py:22
  53.9 1.2 pad_maximum_fusion
  55.1 0.0 copy-start
  55.1 1.1 slice_bitcast_fusion.1
  56.2 0.4 copy-done.9
  56.6 0.2 copy-done.11
  56.8 2.0 %select_maximum_fusion = f32[3,18,8194]{2,1,0:T(8,128)S(1)} fusion(f32[3,1,8192]{2,1,0:T(1,128)} %collective-permute-done.5, f32[3,1,8192]{2,1,0:T(1,128)S(1)} %collective-permute-done.4, f32[1,16,8192]{2,1,0:T(8,128)S(1)} %bitcast.48, f32[1,16,8192]{2,1,0:T(8,128)S(1)} %copy-done.9, f32[1,16,8192]{2,1,0:T(8,128)S(1)} %bitcast.36), kind=kLoop, calls=%fused_computation.2 | loop fusion | flops 5309712 | bytes 3539376 | tf_op jit(solution)/shard_map/concatenate | solution.py:18
  58.8 1.3 slice_bitcast_fusion.4
  60.0 1.0 fusion.4
  61.0 1.2 copy.13
  62.2 0.1 copy-done.3
  62.3 3.9 %fusion.59 = (f32[16,8192]{1,0:T(8,128)S(1)}, f32[16,8192]{1,0:T(8,128)S(1)}, f32[16,8192]{1,0:T(8,128)S(1)}, f32[16,8192]{1,0:T(8,128)S(1)}, f32[16,8192]{1,0:T(8,128)S(1)}, /*index=5*/f32[16,8192]{1,0:T(8,128)S(1)}) fusion(f32[18,8194]{1,0:T(8,128)} %fusion.4, f32[18,8194]{1,0:T(8,128)} %get-tuple-element.32, s32[16,8192]{1,0:T(8,128)} %param.21, ...), kind=kLoop, calls=%fused_computation.116 | loop fusion | flops 5767168 | bytes 9961472 | tf_op jit(solution)/shard_map/jit(_where)/select_n | solution.py:51
  66.2 0.0 copy-start.6
  66.3 6.1 %collective-permute-start.6 = (f32[1,8192]{1,0:T(1,128)S(1)}, f32[1,8192]{1,0:T(1,128)S(1)}, u32[]{:S(2)}, u32[]{:S(2)}) collective-permute-start(f32[1,8192]{1,0:T(1,128)S(1)} %get-tuple-element.54), channel_id=1, source_target_pairs={{0,16},{16,32},{32,48},{48,64},{64,80},{80,96},{96,112},{112,128},... | collective-permute-start | bytes 98312 | tf_op jit(solution)/shard_map/ppermute | solution.py:20
  72.3 2.3 %collective-permute-start.7 = (f32[1,8192]{1,0:T(1,128)S(1)}, f32[1,8192]{1,0:T(1,128)S(1)}, u32[]{:S(2)}, u32[]{:S(2)}) collective-permute-start(f32[1,8192]{1,0:T(1,128)S(1)} %get-tuple-element.55), channel_id=1, source_target_pairs={{16,0},{32,16},{48,32},{64,48},{80,64},{96,80},{112,96},{128,112},... | collective-permute-start | bytes 98312 | tf_op jit(solution)/shard_map/ppermute | solution.py:22
  74.7 0.3 fusion.68
  75.0 3.6 %collective-permute-done.7 = f32[1,8192]{1,0:T(1,128)S(1)} collective-permute-done((f32[1,8192]{1,0:T(1,128)S(1)}, f32[1,8192]{1,0:T(1,128)S(1)}, u32[]{:S(2)}, u32[]{:S(2)}) %collective-permute-start.7) | collective-permute-done | bytes 32800 | tf_op jit(solution)/shard_map/ppermute | solution.py:22
  78.6 0.4 fusion.3
  79.1 0.8 fusion.52
  79.9 2.4 %collective-permute-start.8 = (f32[1,8192]{1,0:T(1,128)S(1)}, f32[1,8192]{1,0:T(1,128)S(1)}, u32[]{:S(2)}, u32[]{:S(2)}) collective-permute-start(f32[1,8192]{1,0:T(1,128)S(1)} %get-tuple-element.52), channel_id=1, source_target_pairs={{0,16},{16,32},{32,48},{48,64},{64,80},{80,96},{96,112},{112,128},... | collective-permute-start | bytes 98312 | tf_op jit(solution)/shard_map/ppermute | solution.py:20
  82.4 5.9 %collective-permute-start.9 = (f32[1,8192]{1,0:T(1,128)S(1)}, f32[1,8192]{1,0:T(1,128)S(1)}, u32[]{:S(2)}, u32[]{:S(2)}) collective-permute-start(f32[1,8192]{1,0:T(1,128)S(1)} %get-tuple-element.53), channel_id=1, source_target_pairs={{16,0},{32,16},{48,32},{64,48},{80,64},{96,80},{112,96},{128,112},... | collective-permute-start | bytes 98312 | tf_op jit(solution)/shard_map/ppermute | solution.py:22
  88.2 0.3 fusion.62
  88.6 0.7 collective-permute-done.9
  89.2 0.4 fusion.2
  89.7 0.8 fusion.45
  90.5 2.4 %collective-permute-start.10 = (f32[1,8192]{1,0:T(1,128)S(1)}, f32[1,8192]{1,0:T(1,128)S(1)}, u32[]{:S(2)}, u32[]{:S(2)}) collective-permute-start(f32[1,8192]{1,0:T(1,128)S(1)} %get-tuple-element.50), channel_id=1, source_target_pairs={{0,16},{16,32},{32,48},{48,64},{64,80},{80,96},{96,112},{112,128},... | collective-permute-start | bytes 98312 | tf_op jit(solution)/shard_map/ppermute | solution.py:20
  92.9 6.6 %collective-permute-start.11 = (f32[1,8192]{1,0:T(1,128)S(1)}, f32[1,8192]{1,0:T(1,128)S(1)}, u32[]{:S(2)}, u32[]{:S(2)}) collective-permute-start(f32[1,8192]{1,0:T(1,128)S(1)} %get-tuple-element.51), channel_id=1, source_target_pairs={{16,0},{32,16},{48,32},{64,48},{80,64},{96,80},{112,96},{128,112},... | collective-permute-start | bytes 98312 | tf_op jit(solution)/shard_map/ppermute | solution.py:22
  99.6 0.8 collective-permute-done.11
  100.4 0.4 fusion.1
  100.8 0.0 copy-start.7
  100.8 0.8 fusion.38
  101.6 0.2 copy-done.7
  101.9 1.4 %fusion.31 = f32[16,16,512]{2,1,0:T(8,128)S(1)} fusion(f32[16,16,512]{2,1,0:T(8,128)S(1)} %fusion.63, f32[16,18,514]{2,1,0:T(8,128)S(1)} %copy-done.2, f32[15,16,512]{2,1,0:T(8,128)S(1)} %get-tuple-element.42, f32[15,16,512]{2,1,0:T(8,128)S(1)} %get-tuple-element.41, f32[15,16,512]{2,1,0:T(8,128)S(1)} %fusion.62, f32[1,16,512]{2,1,0:T(8,128)S(1)} %add_bitcast_fusion, ...), kind=kLoop, calls=%fused_computation.71 | loop fusion | flops 5898240 | bytes 7274496 | tf_op jit(solution)/shard_map/jit(_where)/select_n | solution.py:51
  103.3 0.1 fusion.70
  103.4 6.7 %collective-permute-start.12 = (f32[16,1,512]{2,1,0:T(1,128)S(1)}, f32[16,1,512]{2,1,0:T(1,128)S(1)}, u32[]{:S(2)}, u32[]{:S(2)}) collective-permute-start(f32[16,1,512]{2,1,0:T(1,128)S(1)} %get-tuple-element.48), channel_id=1, source_target_pairs={{16,0},{32,16},{48,32},{64,48},{80,64},{96,80},{112,96},{128,112},... | collective-permute-start | bytes 98312 | tf_op jit(solution)/shard_map/ppermute | solution.py:22
  110.0 1.9 %collective-permute-start.13 = (f32[16,1,512]{2,1,0:T(1,128)S(1)}, f32[16,1,512]{2,1,0:T(1,128)S(1)}, u32[]{:S(2)}, u32[]{:S(2)}) collective-permute-start(f32[16,1,512]{2,1,0:T(1,128)S(1)} %get-tuple-element.47), channel_id=1, source_target_pairs={{0,16},{16,32},{32,48},{48,64},{64,80},{80,96},{96,112},{112,128},... | collective-permute-start | bytes 98312 | tf_op jit(solution)/shard_map/ppermute | solution.py:20
  112.0 5.7 %collective-permute-done.13 = f32[16,1,512]{2,1,0:T(1,128)S(1)} collective-permute-done((f32[16,1,512]{2,1,0:T(1,128)S(1)}, f32[16,1,512]{2,1,0:T(1,128)S(1)}, u32[]{:S(2)}, u32[]{:S(2)}) %collective-permute-start.13) | collective-permute-done | bytes 32800 | tf_op jit(solution)/shard_map/ppermute | solution.py:20
  117.7 0.1 pad_maximum_fusion.15
  117.9 1.9 %collective-permute-start.14 = (f32[16,18,1]{2,1,0:T(8,128)S(1)}, f32[16,18,1]{2,1,0:T(8,128)S(1)}, u32[]{:S(2)}, u32[]{:S(2)}) collective-permute-start(f32[16,18,1]{2,1,0:T(8,128)S(1)} %get-tuple-element.43), channel_id=1, source_target_pairs={{1,0},{2,1},{3,2},{4,3},{5,4},{6,5},{7,6},{8,7},{9,8},{10,9},{11,1... | collective-permute-start | bytes 3464 | tf_op jit(solution)/shard_map/ppermute | solution.py:22
  119.8 7.1 %collective-permute-start.15 = (f32[16,18,1]{2,1,0:T(8,128)S(1)}, f32[16,18,1]{2,1,0:T(8,128)S(1)}, u32[]{:S(2)}, u32[]{:S(2)}) collective-permute-start(f32[16,18,1]{2,1,0:T(8,128)S(1)} %get-tuple-element.44), channel_id=1, source_target_pairs={{0,1},{1,2},{2,3},{3,4},{4,5},{5,6},{6,7},{7,8},{8,9},{9,10},{10,1... | collective-permute-start | bytes 3464 | tf_op jit(solution)/shard_map/ppermute | solution.py:20
  126.9 0.1 fusion.69
  127.1 3.4 %collective-permute-done.14 = f32[16,18,1]{2,1,0:T(8,128)S(1)} collective-permute-done((f32[16,18,1]{2,1,0:T(8,128)S(1)}, f32[16,18,1]{2,1,0:T(8,128)S(1)}, u32[]{:S(2)}, u32[]{:S(2)}) %collective-permute-start.14) | collective-permute-done | bytes 1184 | tf_op jit(solution)/shard_map/ppermute | solution.py:22
  130.4 3.3 %collective-permute-done.15 = f32[16,18,1]{2,1,0:T(8,128)S(1)} collective-permute-done((f32[16,18,1]{2,1,0:T(8,128)S(1)}, f32[16,18,1]{2,1,0:T(8,128)S(1)}, u32[]{:S(2)}, u32[]{:S(2)}) %collective-permute-start.15) | collective-permute-done | bytes 1184 | tf_op jit(solution)/shard_map/ppermute | solution.py:20
  133.7 2.3 %fusion.20 = f32[16,16,512]{2,1,0:T(8,128)} fusion(f32[16,16,512]{2,1,0:T(8,128)S(1)} %fusion.63, f32[16,18,1]{2,1,0:T(8,128)S(1)} %collective-permute-done.15, f32[16,1,512]{2,1,0:T(1,128)S(1)} %collective-permute-done.12, f32[16,16,512]{2,1,0:T(8,128)S(1)} %fusion.31, f32[16,1,512]{2,1,0:T(1,128)S(1)} %collective-permute-done.13, ...), kind=kLoop, calls=%fused_computation.52 | loop fusion | flops 6946816 | bytes 5769472 | tf_op jit(solution)/shard_map/jit(_where)/select_n | solution.py:51
  (36 shorter events, 0.2 us)
Async XLA Ops:
  0.6 12.9 %copy-start.5 = (f32[16,16,512]{2,1,0:T(8,128)S(1)}, f32[16,16,512]{2,1,0:T(8,128)}, u32[]{:S(2)}) copy-start(f32[16,16,512]{2,1,0:T(8,128)} %param.13) | copy-start | bytes 1572868
  0.6 20.2 %copy-start.10 = (f32[16,16,512]{2,1,0:T(8,128)S(1)}, f32[16,16,512]{2,1,0:T(8,128)}, u32[]{:S(2)}) copy-start(f32[16,16,512]{2,1,0:T(8,128)} %param.14) | copy-start | bytes 1572868
  2.2 0.8 copy-start.8
  2.2 27.0 %copy-start.13 = (s32[16,512]{1,0:T(8,128)S(1)}, s32[16,512]{1,0:T(8,128)}, u32[]{:S(2)}) copy-start(s32[16,512]{1,0:T(8,128)} %param.15) | copy-start | bytes 98308
  2.2 27.1 %copy-start.14 = (s32[16,512]{1,0:T(8,128)S(1)}, s32[16,512]{1,0:T(8,128)}, u32[]{:S(2)}) copy-start(s32[16,512]{1,0:T(8,128)} %param.16) | copy-start | bytes 98308
  2.2 27.1 %copy-start.15 = (f32[17]{0:T(128)S(1)}, f32[17]{0:T(128)}, u32[]{:S(2)}) copy-start(f32[17]{0:T(128)} %param.17) | copy-start | bytes 208
  4.3 51.9 %collective-permute-start.4 = (f32[3,1,8192]{2,1,0:T(1,128)S(1)}, f32[3,1,8192]{2,1,0:T(1,128)S(1)}, u32[]{:S(2)}, u32[]{:S(2)}) collective-permute-start(f32[3,1,8192]{2,1,0:T(1,128)S(1)} %get-tuple-element.35), channel_id=1, source_target_pairs={{0,16},{16,32},{32,48},{48,64},{64,80},{80,96},{96,112},{112,128},... | collective-permute-start | bytes 294920 | tf_op jit(solution)/shard_map/ppermute | solution.py:20
  9.2 46.9 %collective-permute-start.5 = (f32[3,1,8192]{2,1,0:T(1,128)S(1)}, f32[3,1,8192]{2,1,0:T(1,128)}, u32[]{:S(2)}, u32[]{:S(2)}) collective-permute-start(f32[3,1,8192]{2,1,0:T(1,128)S(1)} %get-tuple-element.36), channel_id=1, source_target_pairs={{16,0},{32,16},{48,32},{64,48},{80,64},{96,80},{112,96},{128,112},... | collective-permute-start | bytes 294920 | tf_op jit(solution)/shard_map/ppermute | solution.py:22
  14.4 46.6 %all-to-all-start = ((f32[16,16,512]{2,1,0:T(8,128)}), f32[16,16,512]{2,1,0:T(8,128)}, u32[]{:S(2)}, u32[]{:S(2)}) async-start(f32[16,16,512]{2,1,0:T(8,128)} %stack.31), calls=%async_computation | async-start | bytes 1048576 | tf_op jit(solution)/shard_map/all_to_all | solution.py:90
  21.0 8.5 %collective-permute-start = (f32[2,16,1,512]{3,2,1,0:T(1,128)S(1)}, f32[2,16,1,512]{3,2,1,0:T(1,128)S(1)}, u32[]{:S(2)}, u32[]{:S(2)}) collective-permute-start(f32[2,16,1,512]{3,2,1,0:T(1,128)S(1)} %get-tuple-element.39), channel_id=1, source_target_pairs={{0,16},{16,32},{32,48},{48,64},{64,80},{80,96},{96,112},{112,128},... | collective-permute-start | bytes 196616 | tf_op jit(solution)/shard_map/ppermute | solution.py:20
  23.8 7.5 %collective-permute-start.1 = (f32[2,16,1,512]{3,2,1,0:T(1,128)S(1)}, f32[2,16,1,512]{3,2,1,0:T(1,128)S(1)}, u32[]{:S(2)}, u32[]{:S(2)}) collective-permute-start(f32[2,16,1,512]{3,2,1,0:T(1,128)S(1)} %get-tuple-element.40), channel_id=1, source_target_pairs={{16,0},{32,16},{48,32},{64,48},{80,64},{96,80},{112,96},{128,112},... | collective-permute-start | bytes 196616 | tf_op jit(solution)/shard_map/ppermute | solution.py:22
  31.5 14.8 %collective-permute-start.2 = (f32[2,16,18,1]{3,2,1,0:T(8,128)S(1)}, f32[2,16,18,1]{3,2,1,0:T(8,128)S(1)}, u32[]{:S(2)}, u32[]{:S(2)}) collective-permute-start(f32[2,16,18,1]{3,2,1,0:T(8,128)S(1)} %get-tuple-element.37), channel_id=1, source_target_pairs={{0,1},{1,2},{2,3},{3,4},{4,5},{5,6},{6,7},{7,8},{8,9},{9,10},{10,1... | collective-permute-start | bytes 6920 | tf_op jit(solution)/shard_map/ppermute | solution.py:20
  37.5 16.4 %collective-permute-start.3 = (f32[2,16,18,1]{3,2,1,0:T(8,128)S(1)}, f32[2,16,18,1]{3,2,1,0:T(8,128)S(1)}, u32[]{:S(2)}, u32[]{:S(2)}) collective-permute-start(f32[2,16,18,1]{3,2,1,0:T(8,128)S(1)} %get-tuple-element.38), channel_id=1, source_target_pairs={{1,0},{2,1},{3,2},{4,3},{5,4},{6,5},{7,6},{8,7},{9,8},{10,9},{11,1... | collective-permute-start | bytes 6920 | tf_op jit(solution)/shard_map/ppermute | solution.py:22
  55.1 1.1 copy-start
  55.1 1.5 %copy-start.9 = (f32[1,16,8192]{2,1,0:T(8,128)S(1)}, f32[1,16,8192]{2,1,0:T(8,128)}, u32[]{:S(2)}) copy-start(f32[1,16,8192]{2,1,0:T(8,128)} %copy-done.8) | copy-start | bytes 1572868
  55.1 1.7 %copy-start.11 = (f32[16,8192]{1,0:T(8,128)S(1)}, f32[16,8192]{1,0:T(8,128)}, u32[]{:S(2)}) copy-start(f32[16,8192]{1,0:T(8,128)} %param.20) | copy-start | bytes 1572868
  61.0 1.3 copy-start.3
  62.3 12.4 %copy-start.2 = (f32[16,18,514]{2,1,0:T(8,128)S(1)}, f32[16,18,514]{2,1,0:T(8,128)}, u32[]{:S(2)}) copy-start(f32[16,18,514]{2,1,0:T(8,128)} %get-tuple-element.34) | copy-start | bytes 1776388
  66.2 12.9 %copy-start.1 = (f32[16,8192]{1,0:T(8,128)S(1)}, f32[16,8192]{1,0:T(8,128)}, u32[]{:S(2)}) copy-start(f32[16,8192]{1,0:T(8,128)} %param.18) | copy-start | bytes 1572868
  66.2 12.9 %copy-start.4 = (f32[18,8194]{1,0:T(8,128)S(1)}, f32[18,8194]{1,0:T(8,128)}, u32[]{:S(2)}) copy-start(f32[18,8194]{1,0:T(8,128)} %get-tuple-element.32) | copy-start | bytes 1769908
  66.2 12.9 %copy-start.6 = (s32[16,8192]{1,0:T(8,128)S(1)}, s32[16,8192]{1,0:T(8,128)}, u32[]{:S(2)}) copy-start(s32[16,8192]{1,0:T(8,128)} %param.21) | copy-start | bytes 1572868
  66.3 8.8 %collective-permute-start.6 = (f32[1,8192]{1,0:T(1,128)S(1)}, f32[1,8192]{1,0:T(1,128)S(1)}, u32[]{:S(2)}, u32[]{:S(2)}) collective-permute-start(f32[1,8192]{1,0:T(1,128)S(1)} %get-tuple-element.54), channel_id=1, source_target_pairs={{0,16},{16,32},{32,48},{48,64},{64,80},{80,96},{96,112},{112,128},... | collective-permute-start | bytes 98312 | tf_op jit(solution)/shard_map/ppermute | solution.py:20
  72.3 6.3 %collective-permute-start.7 = (f32[1,8192]{1,0:T(1,128)S(1)}, f32[1,8192]{1,0:T(1,128)S(1)}, u32[]{:S(2)}, u32[]{:S(2)}) collective-permute-start(f32[1,8192]{1,0:T(1,128)S(1)} %get-tuple-element.55), channel_id=1, source_target_pairs={{16,0},{32,16},{48,32},{64,48},{80,64},{96,80},{112,96},{128,112},... | collective-permute-start | bytes 98312 | tf_op jit(solution)/shard_map/ppermute | solution.py:22
  79.9 8.6 %collective-permute-start.8 = (f32[1,8192]{1,0:T(1,128)S(1)}, f32[1,8192]{1,0:T(1,128)S(1)}, u32[]{:S(2)}, u32[]{:S(2)}) collective-permute-start(f32[1,8192]{1,0:T(1,128)S(1)} %get-tuple-element.52), channel_id=1, source_target_pairs={{0,16},{16,32},{32,48},{48,64},{64,80},{80,96},{96,112},{112,128},... | collective-permute-start | bytes 98312 | tf_op jit(solution)/shard_map/ppermute | solution.py:20
  82.4 6.9 %collective-permute-start.9 = (f32[1,8192]{1,0:T(1,128)S(1)}, f32[1,8192]{1,0:T(1,128)S(1)}, u32[]{:S(2)}, u32[]{:S(2)}) collective-permute-start(f32[1,8192]{1,0:T(1,128)S(1)} %get-tuple-element.53), channel_id=1, source_target_pairs={{16,0},{32,16},{48,32},{64,48},{80,64},{96,80},{112,96},{128,112},... | collective-permute-start | bytes 98312 | tf_op jit(solution)/shard_map/ppermute | solution.py:22
  90.5 9.1 %collective-permute-start.10 = (f32[1,8192]{1,0:T(1,128)S(1)}, f32[1,8192]{1,0:T(1,128)S(1)}, u32[]{:S(2)}, u32[]{:S(2)}) collective-permute-start(f32[1,8192]{1,0:T(1,128)S(1)} %get-tuple-element.50), channel_id=1, source_target_pairs={{0,16},{16,32},{32,48},{48,64},{64,80},{80,96},{96,112},{112,128},... | collective-permute-start | bytes 98312 | tf_op jit(solution)/shard_map/ppermute | solution.py:20
  92.9 7.4 %collective-permute-start.11 = (f32[1,8192]{1,0:T(1,128)S(1)}, f32[1,8192]{1,0:T(1,128)S(1)}, u32[]{:S(2)}, u32[]{:S(2)}) collective-permute-start(f32[1,8192]{1,0:T(1,128)S(1)} %get-tuple-element.51), channel_id=1, source_target_pairs={{16,0},{32,16},{48,32},{64,48},{80,64},{96,80},{112,96},{128,112},... | collective-permute-start | bytes 98312 | tf_op jit(solution)/shard_map/ppermute | solution.py:22
  100.8 1.0 copy-start.7
  101.8 1.4 %copy-start.12 = (f32[16,8192]{1,0:T(8,128)}, f32[16,8192]{1,0:T(8,128)S(1)}, u32[]{:S(2)}) copy-start(f32[16,8192]{1,0:T(8,128)S(1)} %fusion.38) | copy-start | bytes 1572868
  103.4 8.6 %collective-permute-start.12 = (f32[16,1,512]{2,1,0:T(1,128)S(1)}, f32[16,1,512]{2,1,0:T(1,128)S(1)}, u32[]{:S(2)}, u32[]{:S(2)}) collective-permute-start(f32[16,1,512]{2,1,0:T(1,128)S(1)} %get-tuple-element.48), channel_id=1, source_target_pairs={{16,0},{32,16},{48,32},{64,48},{80,64},{96,80},{112,96},{128,112},... | collective-permute-start | bytes 98312 | tf_op jit(solution)/shard_map/ppermute | solution.py:22
  110.0 7.7 %collective-permute-start.13 = (f32[16,1,512]{2,1,0:T(1,128)S(1)}, f32[16,1,512]{2,1,0:T(1,128)S(1)}, u32[]{:S(2)}, u32[]{:S(2)}) collective-permute-start(f32[16,1,512]{2,1,0:T(1,128)S(1)} %get-tuple-element.47), channel_id=1, source_target_pairs={{0,16},{16,32},{32,48},{48,64},{64,80},{80,96},{96,112},{112,128},... | collective-permute-start | bytes 98312 | tf_op jit(solution)/shard_map/ppermute | solution.py:20
  117.9 12.6 %collective-permute-start.14 = (f32[16,18,1]{2,1,0:T(8,128)S(1)}, f32[16,18,1]{2,1,0:T(8,128)S(1)}, u32[]{:S(2)}, u32[]{:S(2)}) collective-permute-start(f32[16,18,1]{2,1,0:T(8,128)S(1)} %get-tuple-element.43), channel_id=1, source_target_pairs={{1,0},{2,1},{3,2},{4,3},{5,4},{6,5},{7,6},{8,7},{9,8},{10,9},{11,1... | collective-permute-start | bytes 3464 | tf_op jit(solution)/shard_map/ppermute | solution.py:22
  119.8 13.9 %collective-permute-start.15 = (f32[16,18,1]{2,1,0:T(8,128)S(1)}, f32[16,18,1]{2,1,0:T(8,128)S(1)}, u32[]{:S(2)}, u32[]{:S(2)}) collective-permute-start(f32[16,18,1]{2,1,0:T(8,128)S(1)} %get-tuple-element.44), channel_id=1, source_target_pairs={{0,1},{1,2},{2,3},{3,4},{4,5},{5,6},{6,7},{7,8},{8,9},{9,10},{10,1... | collective-permute-start | bytes 3464 | tf_op jit(solution)/shard_map/ppermute | solution.py:20
